TPU v7x, 512 devices: a whole 4x4x16 slice. The times are simulated.
512 devices in a mesh: dp: 8 (over y, core), expert: 64 (over x, z).
Axes of the slice: x: 4, y: 4, z: 16, core: 2. Of those that a mesh axis runs over, the one named last changes fastest.
Arguments:
- layer_in: bfloat16 [2048, 4096], P('expert', 'dp'), may hold values from -6 to 6
- grad_out: bfloat16 [2048, 4096], P('expert', 'dp'), may hold values from -6 to 6
- gate_prob: float32 [2048, 8], P('expert'), may hold values from 0.05 to 0.6
- expert_ids: int32 [2048, 8], P('expert'), may hold values from 0 to 31, as said below
- replica_index: int32 [2048, 8], P('expert'), may hold values from 0 to 3, as said below
- slot_expert: int32 [64], replicated, may hold values from 0 to 31, as said below
- w_gate: bfloat16 [64, 4096, 1024], P('expert', None, 'dp')
- w_up: bfloat16 [64, 4096, 1024], P('expert', None, 'dp')
- w_down: bfloat16 [64, 1024, 4096], P('expert', 'dp')
Outputs:
- grad_in: bfloat16 [2048, 4096], P('expert', 'dp')
- grad_w_down: bfloat16 [64, 1024, 4096], P('expert', 'dp')
Inputs may be any that keep to these rules, and one draw needn't show every extreme that they name: `slot_expert`: every expert owns one run of consecutive slots, counted cyclically (slot 63 is followed by slot 0), of 1 to 4 slots; the runs cover all 64 slots. `expert_ids`: the 8 experts of one token are different. `replica_index`: each entry is below the number of slots of the expert of the same choice. Of the 32 tokens of one index of expert, at most 8 choices go to any one slot, and in every draw some slot receives exactly 8 from the tokens of every index of expert.
All inputs are finite; a program needn't handle non-finite values.
Results may differ from a plain program's by a relative error of at most 0.014.
Values may be sent and summed in bfloat16 or wider, within the bound.
No kernel may reach another device: no remote copies, remote signals or barrier semaphores. Data moves between devices by JAX's collectives and lax.ppermute only.
A program may use at most 64 MiB of HBM per device.

v0:
```python
import jax
import jax.numpy as jnp
from jax import lax
from jax.sharding import PartitionSpec as P

TOP = 8


def passed_along(value, axis, steps):
    count = lax.axis_size(axis)
    pairs = [(source, (source + steps) % count) for source in range(count)]
    return lax.ppermute(value, axis, pairs)


def body(
    layer_in, grad_out, gate_prob, expert_ids, replica_index, slot_expert, w_gate, w_up, w_down
):
    slots = lax.axis_size("expert")
    maxrep = min(4, slots // 8)
    tok_count = layer_in.shape[0]
    capacity = tok_count // maxrep
    recv_rows = slots * capacity
    expert_count = (8 - maxrep) * slots // 8
    slot_index = jnp.arange(slots, dtype=jnp.int32)
    expert_index = jnp.arange(expert_count, dtype=jnp.int32)
    is_start = slot_expert != jnp.roll(slot_expert, 1)
    first_slot = jnp.sum(
        jnp.where(
            (slot_expert[None, :] == expert_index[:, None]) & is_start[None, :],
            slot_index[None, :],
            0,
        ),
        axis=1,
    )
    expert_flat = expert_ids.reshape(-1)
    route_slot = jnp.sum(
        jnp.where(expert_flat[:, None] == expert_index[None, :], first_slot[None, :], 0), axis=1
    )
    route_slot = (route_slot + replica_index.reshape(-1)) % slots
    onehot = (route_slot[:, None] == slot_index[None, :]).astype(jnp.int32)
    rank_in_slot = jnp.sum((jnp.cumsum(onehot, axis=0) - onehot) * onehot, axis=1)
    position = route_slot * capacity + rank_in_slot
    prob_flat = gate_prob.reshape(-1)

    def pack(values):
        buffer = jnp.zeros((recv_rows, values.shape[1]), values.dtype).at[position].set(values)
        return buffer.reshape(slots, capacity, values.shape[1])

    repeated = jnp.repeat(grad_out, TOP, axis=0).astype(jnp.float32)
    inputs, scaled = (
        lax.all_gather(
            lax.all_to_all(
                pack(jnp.repeat(layer_in, TOP, axis=0)),
                "expert",
                split_axis=0,
                concat_axis=0,
                tiled=True,
            ),
            "dp",
            axis=2,
            tiled=True,
        ),
        lax.all_gather(
            lax.all_to_all(
                pack((prob_flat[:, None] * repeated).astype(jnp.bfloat16)),
                "expert",
                split_axis=0,
                concat_axis=0,
                tiled=True,
            ),
            "dp",
            axis=2,
            tiled=True,
        ),
    )
    inputs = inputs.reshape(recv_rows, -1)
    scaled = scaled.reshape(recv_rows, -1)
    width = inputs.shape[1]
    gate_matrix = w_gate[0]
    up_matrix = w_up[0]
    down_matrix = w_down[0]
    gate_pre = jnp.dot(inputs, gate_matrix, preferred_element_type=jnp.float32)
    up_pre = jnp.dot(inputs, up_matrix, preferred_element_type=jnp.float32)
    hidden = (jax.nn.silu(gate_pre) * up_pre).astype(jnp.bfloat16)
    contract_last = (((1,), (1,)), ((), ()))
    hidden_grad = lax.dot_general(
        scaled, down_matrix, contract_last, preferred_element_type=jnp.float32
    )
    sigma = jax.nn.sigmoid(gate_pre)
    gate_grad = (hidden_grad * up_pre * sigma * (1.0 + gate_pre * (1.0 - sigma))).astype(
        jnp.bfloat16
    )
    up_grad = (hidden_grad * gate_pre * sigma).astype(jnp.bfloat16)
    partial_value = lax.dot_general(
        gate_grad, gate_matrix, contract_last, preferred_element_type=jnp.float32
    )
    partial_value = partial_value + lax.dot_general(
        up_grad, up_matrix, contract_last, preferred_element_type=jnp.float32
    )
    partial_value = partial_value.reshape(slots, capacity, width)
    summed = lax.psum_scatter(
        partial_value.astype(jnp.bfloat16), "dp", scatter_dimension=2, tiled=True
    ).astype(jnp.float32)
    returned = lax.all_to_all(
        summed.astype(jnp.bfloat16), "expert", split_axis=0, concat_axis=0, tiled=True
    ).astype(summed.dtype)
    flat_back = returned.reshape(recv_rows, -1)
    grad_in = jnp.sum(flat_back[position].reshape(tok_count, TOP, -1), axis=1).astype(jnp.bfloat16)
    slot_partial = lax.dot_general(
        hidden, scaled, (((0,), (0,)), ((), ())), preferred_element_type=jnp.float32
    ).astype(jnp.bfloat16)
    own_index = lax.axis_index("expert")
    expert_here = jnp.sum(jnp.where(slot_index == own_index, slot_expert, 0))

    def same_at(offset):
        neighbour = (own_index - offset) % slots
        match = jnp.any((slot_index == neighbour) & (slot_expert == expert_here))
        return match.astype(jnp.float32)

    total = slot_partial.astype(jnp.float32)
    for distance in range(1, maxrep):
        from_left = passed_along(slot_partial, "expert", distance)
        from_right = passed_along(slot_partial, "expert", -distance)
        total = (
            total
            + same_at(distance) * from_left.astype(jnp.float32)
            + same_at(-distance) * from_right.astype(jnp.float32)
        )
    grad_w_down = total.astype(jnp.bfloat16)[None]
    return (grad_in, grad_w_down)


def solution(mesh):
    placed = (
        P("expert", "dp"),
        P("expert", "dp"),
        P("expert", None),
        P("expert", None),
        P("expert", None),
        P(),
        P("expert", None, "dp"),
        P("expert", None, "dp"),
        P("expert", "dp", None),
    )
    return jax.shard_map(
        body,
        mesh=mesh,
        in_specs=placed,
        out_specs=(P("expert", "dp"), P("expert", "dp", None)),
        check_vma=False,
    )
```

profile of v0, /device:TPU:32, one launch (start us, length us, event | category | flops | bytes accessed | tf_op | source)
XLA Modules:
  0.0 336.8 jit_solution(1470478465016000383)
XLA Ops:
  10.9 2.1 broadcast_compare_fusion
  15.7 1.9 scatter_custom_fusion.1
  17.6 49.0 %all_to_all.15 = bf16[64,8,512]{2,1,0:T(8,128)(2,1)} all-to-all(bf16[64,8,512]{2,1,0:T(8,128)(2,1)S(1)} %bitcast.69), channel_id=1, replica_groups=mesh['dp'=8,'expert'=64] {'expert'}, dimensions={0} | all-to-all | bytes 1048576 | tf_op jit(solution)/shard_map/all_to_all | solution.py:52
  66.9 1.7 scatter_custom_fusion
  68.7 38.0 %all_to_all.16 = bf16[64,8,512]{2,1,0:T(8,128)(2,1)} all-to-all(bf16[64,8,512]{2,1,0:T(8,128)(2,1)S(1)} %bitcast.70), channel_id=1, replica_groups=mesh['dp'=8,'expert'=64] {'expert'}, dimensions={0} | all-to-all | bytes 1048576 | tf_op jit(solution)/shard_map/all_to_all | solution.py:64
  106.8 3.6 %fusion.1 = f32[512,128]{1,0:T(8,128)S(1)} fusion(bf16[64,8,4096]{2,1,0:T(8,128)(2,1)} %all-gather.5.cloned.1.call-done, bf16[1,4096,128]{2,1,0:T(8,128)(2,1)S(1)} %copy-done), kind=kOutput, calls=%fused_computation.6 | convolution fusion | flops 536870912 | bytes 5505024 | tf_op jit(solution)/shard_map/dot_general | solution.py:82
  111.7 30.4 %all-gather.3.cloned.1.call-done = bf16[64,8,4096]{2,1,0:T(8,128)(2,1)} async-done(((bf16[64,8,512]{2,1,0:T(8,128)(2,1)}), bf16[64,8,4096]{2,1,0:T(8,128)(2,1)}) %all-gather.3.cloned.1.call-update) | async-done | bytes 4194320 | tf_op jit(solution)/shard_map/all_gather | solution.py:63
  142.2 3.7 %fusion.6 = f32[512,128]{1,0:T(8,128)S(1)} fusion(bf16[64,8,4096]{2,1,0:T(8,128)(2,1)} %all-gather.3.cloned.1.call-done, bf16[1,128,4096]{2,1,0:T(8,128)(2,1)} %param.17), kind=kOutput, calls=%fused_computation.11 | convolution fusion | flops 536870912 | bytes 5505024 | tf_op jit(solution)/shard_map/dot_general | solution.py:86
  147.2 3.2 fusion
  150.4 3.0 convolution_convert_fusion
  153.4 3.6 %collective-permute-start = (bf16[128,4096]{1,0:T(8,128)(2,1)S(1)}, bf16[128,4096]{1,0:T(8,128)(2,1)S(1)}, u32[]{:S(2)}, u32[]{:S(2)}) collective-permute-start(bf16[128,4096]{1,0:T(8,128)(2,1)S(1)} %convolution_convert_fusion), channel_id=1, source_target_pairs={{0,1},{1,2},{2,3},{3,4},{4,5},{5,6},{6,7},{7,8},{8,9},{9,10},{10,1... | collective-permute-start | bytes 3145736 | tf_op jit(solution)/shard_map/ppermute | solution.py:12
  157.1 2.4 collective-permute-start.1
  159.4 5.2 %collective-permute-start.2 = (bf16[128,4096]{1,0:T(8,128)(2,1)S(1)}, bf16[128,4096]{1,0:T(8,128)(2,1)}, u32[]{:S(2)}, u32[]{:S(2)}) collective-permute-start(bf16[128,4096]{1,0:T(8,128)(2,1)S(1)} %convolution_convert_fusion), channel_id=1, source_target_pairs={{0,2},{1,3},{2,4},{3,5},{4,6},{5,7},{6,8},{7,9},{8,10},{9,11},{10,... | collective-permute-start | bytes 3145736 | tf_op jit(solution)/shard_map/ppermute | solution.py:12
  164.6 4.9 %collective-permute-start.3 = (bf16[128,4096]{1,0:T(8,128)(2,1)S(1)}, bf16[128,4096]{1,0:T(8,128)(2,1)}, u32[]{:S(2)}, u32[]{:S(2)}) collective-permute-start(bf16[128,4096]{1,0:T(8,128)(2,1)S(1)} %convolution_convert_fusion), channel_id=1, source_target_pairs={{0,62},{1,63},{2,0},{3,1},{4,2},{5,3},{6,4},{7,5},{8,6},{9,7},{10,... | collective-permute-start | bytes 3145736 | tf_op jit(solution)/shard_map/ppermute | solution.py:12
  169.5 5.8 %collective-permute-start.4 = (bf16[128,4096]{1,0:T(8,128)(2,1)S(1)}, bf16[128,4096]{1,0:T(8,128)(2,1)}, u32[]{:S(2)}, u32[]{:S(2)}) collective-permute-start(bf16[128,4096]{1,0:T(8,128)(2,1)S(1)} %convolution_convert_fusion), channel_id=1, source_target_pairs={{0,3},{1,4},{2,5},{3,6},{4,7},{5,8},{6,9},{7,10},{8,11},{9,12},{10... | collective-permute-start | bytes 3145736 | tf_op jit(solution)/shard_map/ppermute | solution.py:12
  175.3 7.0 %collective-permute-done = bf16[128,4096]{1,0:T(8,128)(2,1)S(1)} collective-permute-done((bf16[128,4096]{1,0:T(8,128)(2,1)S(1)}, bf16[128,4096]{1,0:T(8,128)(2,1)S(1)}, u32[]{:S(2)}, u32[]{:S(2)}) %collective-permute-start) | collective-permute-done | bytes 1048608 | tf_op jit(solution)/shard_map/ppermute | solution.py:12
  183.3 8.3 %collective-permute-start.5 = (bf16[128,4096]{1,0:T(8,128)(2,1)S(1)}, bf16[128,4096]{1,0:T(8,128)(2,1)}, u32[]{:S(2)}, u32[]{:S(2)}) collective-permute-start(bf16[128,4096]{1,0:T(8,128)(2,1)S(1)} %convolution_convert_fusion), channel_id=1, source_target_pairs={{0,61},{1,62},{2,63},{3,0},{4,1},{5,2},{6,3},{7,4},{8,5},{9,6},{10... | collective-permute-start | bytes 3145736 | tf_op jit(solution)/shard_map/ppermute | solution.py:12
  191.6 4.8 %reduce-scatter.2.cloned.1.call-done = bf16[64,8,512]{2,1,0:T(8,128)(2,1)} async-done(((bf16[64,8,4096]{2,1,0:T(8,128)(2,1)}), bf16[64,8,512]{2,1,0:T(8,128)(2,1)}) %reduce-scatter.2.cloned.1.call-update) | async-done | bytes 524304 | tf_op jit(solution)/shard_map/reduce_scatter | solution.py:101
  196.4 16.3 %all-to-all-start.2 = ((bf16[64,8,512]{2,1,0:T(8,128)(2,1)}), bf16[64,8,512]{2,1,0:T(8,128)(2,1)S(1)}, u32[]{:S(2)}, u32[]{:S(2)}) async-start(bf16[64,8,512]{2,1,0:T(8,128)(2,1)} %reduce-scatter.2.cloned.1.call-done), calls=%async_computation.3 | async-start | bytes 1048576 | tf_op jit(solution)/shard_map/all_to_all | solution.py:104
  217.4 13.9 %collective-permute-done.2 = bf16[128,4096]{1,0:T(8,128)(2,1)} collective-permute-done((bf16[128,4096]{1,0:T(8,128)(2,1)S(1)}, bf16[128,4096]{1,0:T(8,128)(2,1)}, u32[]{:S(2)}, u32[]{:S(2)}) %collective-permute-start.2) | collective-permute-done | bytes 1048608 | tf_op jit(solution)/shard_map/ppermute | solution.py:12
  231.3 68.1 %collective-permute-done.4 = bf16[128,4096]{1,0:T(8,128)(2,1)} collective-permute-done((bf16[128,4096]{1,0:T(8,128)(2,1)S(1)}, bf16[128,4096]{1,0:T(8,128)(2,1)}, u32[]{:S(2)}, u32[]{:S(2)}) %collective-permute-start.4) | collective-permute-done | bytes 1048608 | tf_op jit(solution)/shard_map/ppermute | solution.py:12
  299.4 8.3 %collective-permute-done.5 = bf16[128,4096]{1,0:T(8,128)(2,1)} collective-permute-done((bf16[128,4096]{1,0:T(8,128)(2,1)S(1)}, bf16[128,4096]{1,0:T(8,128)(2,1)}, u32[]{:S(2)}, u32[]{:S(2)}) %collective-permute-start.5) | collective-permute-done | bytes 1048608 | tf_op jit(solution)/shard_map/ppermute | solution.py:12
  307.7 5.1 %fusion.14 = bf16[1,128,4096]{2,1,0:T(8,128)(2,1)} fusion(bf16[128,4096]{1,0:T(8,128)(2,1)} %collective-permute-done.5, f32[]{:T(128)S(6)} %convert_element_type.106, bf16[128,4096]{1,0:T(8,128)(2,1)} %collective-permute-done.4, f32[]{:T(128)S(6)} %convert_element_type.104, bf16[128,4096]{1,0:T(8,128)(2,1)} %collective-permute-done.3, ...), kind=kLoop, calls=%fused_computation.20 | loop fusion | flops 10485760 | bytes 8388632 | tf_op jit(solution)/shard_map/broadcast_in_dim | solution.py:129
  312.9 15.5 %all-to-all-done.2 = bf16[64,8,512]{2,1,0:T(8,128)(2,1)S(1)} async-done(((bf16[64,8,512]{2,1,0:T(8,128)(2,1)}), bf16[64,8,512]{2,1,0:T(8,128)(2,1)S(1)}, u32[]{:S(2)}, u32[]{:S(2)}) %all-to-all-start.2) | async-done | bytes 524320 | tf_op jit(solution)/shard_map/all_to_all | solution.py:104
  (50 shorter events, 12.9 us)
Async XLA Ops:
  7.2 99.6 %copy-start = (bf16[1,4096,128]{2,1,0:T(8,128)(2,1)S(1)}, bf16[1,4096,128]{2,1,0:T(8,128)(2,1)}, u32[]{:S(2)}) copy-start(bf16[1,4096,128]{2,1,0:T(8,128)(2,1)} %param.15) | copy-start | bytes 3145732
  7.2 59.5 %copy-start.4 = (bf16[32,512]{1,0:T(8,128)(2,1)S(1)}, bf16[32,512]{1,0:T(8,128)(2,1)}, u32[]{:S(2)}) copy-start(bf16[32,512]{1,0:T(8,128)(2,1)} %param.10) | copy-start | bytes 98308
  7.2 59.6 %copy-start.5 = (f32[32,8]{0,1:T(8,128)S(1)}, f32[32,8]{0,1:T(8,128)}, u32[]{:S(2)}) copy-start(f32[32,8]{0,1:T(8,128)} %param.11) | copy-start | bytes 3076
  7.2 99.6 %all-gather.5.cloned.1.call-start = ((), (), s32[]{:S(2)}) async-start(), calls=%async_computation.5 | async-start | bytes 4718592 | tf_op jit(solution)/shard_map/all_gather | solution.py:51
  66.7 75.5 %all-gather.3.cloned.1.call-start = ((), (), s32[]{:S(2)}) async-start(), calls=%async_computation.4 | async-start | bytes 4718592 | tf_op jit(solution)/shard_map/all_gather | solution.py:63
  106.7 3.7 %copy-start.2 = (bf16[1,4096,128]{2,1,0:T(8,128)(2,1)S(1)}, bf16[1,4096,128]{2,1,0:T(8,128)(2,1)}, u32[]{:S(2)}) copy-start(bf16[1,4096,128]{2,1,0:T(8,128)(2,1)} %param.16) | copy-start | bytes 3145732
  106.7 89.7 %reduce-scatter.2.cloned.1.call-start = ((), (), s32[]{:S(2)}) async-start(), calls=%async_computation.6 | async-start | bytes 4718592 | tf_op jit(solution)/shard_map/reduce_scatter | solution.py:101
  106.8 3.7 %copy-start.1 = (bf16[64,8,4096]{2,1,0:T(8,128)(2,1)S(1)}, bf16[64,8,4096]{2,1,0:T(8,128)(2,1)}, u32[]{:S(2)}) copy-start(bf16[64,8,4096]{2,1,0:T(8,128)(2,1)} %all-gather.5.cloned.1.call-done) | copy-start | bytes 12582916
  153.4 28.9 %collective-permute-start = (bf16[128,4096]{1,0:T(8,128)(2,1)S(1)}, bf16[128,4096]{1,0:T(8,128)(2,1)S(1)}, u32[]{:S(2)}, u32[]{:S(2)}) collective-permute-start(bf16[128,4096]{1,0:T(8,128)(2,1)S(1)} %convolution_convert_fusion), channel_id=1, source_target_pairs={{0,1},{1,2},{2,3},{3,4},{4,5},{5,6},{6,7},{7,8},{8,9},{9,10},{10,1... | collective-permute-start | bytes 3145736 | tf_op jit(solution)/shard_map/ppermute | solution.py:12
  157.1 60.3 %collective-permute-start.1 = (bf16[128,4096]{1,0:T(8,128)(2,1)S(1)}, bf16[128,4096]{1,0:T(8,128)(2,1)}, u32[]{:S(2)}, u32[]{:S(2)}) collective-permute-start(bf16[128,4096]{1,0:T(8,128)(2,1)S(1)} %convolution_convert_fusion), channel_id=1, source_target_pairs={{0,63},{1,0},{2,1},{3,2},{4,3},{5,4},{6,5},{7,6},{8,7},{9,8},{10,9... | collective-permute-start | bytes 3145736 | tf_op jit(solution)/shard_map/ppermute | solution.py:12
  159.4 71.9 %collective-permute-start.2 = (bf16[128,4096]{1,0:T(8,128)(2,1)S(1)}, bf16[128,4096]{1,0:T(8,128)(2,1)}, u32[]{:S(2)}, u32[]{:S(2)}) collective-permute-start(bf16[128,4096]{1,0:T(8,128)(2,1)S(1)} %convolution_convert_fusion), channel_id=1, source_target_pairs={{0,2},{1,3},{2,4},{3,5},{4,6},{5,7},{6,8},{7,9},{8,10},{9,11},{10,... | collective-permute-start | bytes 3145736 | tf_op jit(solution)/shard_map/ppermute | solution.py:12
  164.6 66.7 %collective-permute-start.3 = (bf16[128,4096]{1,0:T(8,128)(2,1)S(1)}, bf16[128,4096]{1,0:T(8,128)(2,1)}, u32[]{:S(2)}, u32[]{:S(2)}) collective-permute-start(bf16[128,4096]{1,0:T(8,128)(2,1)S(1)} %convolution_convert_fusion), channel_id=1, source_target_pairs={{0,62},{1,63},{2,0},{3,1},{4,2},{5,3},{6,4},{7,5},{8,6},{9,7},{10,... | collective-permute-start | bytes 3145736 | tf_op jit(solution)/shard_map/ppermute | solution.py:12
  169.5 129.9 %collective-permute-start.4 = (bf16[128,4096]{1,0:T(8,128)(2,1)S(1)}, bf16[128,4096]{1,0:T(8,128)(2,1)}, u32[]{:S(2)}, u32[]{:S(2)}) collective-permute-start(bf16[128,4096]{1,0:T(8,128)(2,1)S(1)} %convolution_convert_fusion), channel_id=1, source_target_pairs={{0,3},{1,4},{2,5},{3,6},{4,7},{5,8},{6,9},{7,10},{8,11},{9,12},{10... | collective-permute-start | bytes 3145736 | tf_op jit(solution)/shard_map/ppermute | solution.py:12
  182.3 1.0 copy-start.3
  183.3 124.4 %collective-permute-start.5 = (bf16[128,4096]{1,0:T(8,128)(2,1)S(1)}, bf16[128,4096]{1,0:T(8,128)(2,1)}, u32[]{:S(2)}, u32[]{:S(2)}) collective-permute-start(bf16[128,4096]{1,0:T(8,128)(2,1)S(1)} %convolution_convert_fusion), channel_id=1, source_target_pairs={{0,61},{1,62},{2,63},{3,0},{4,1},{5,2},{6,3},{7,4},{8,5},{9,6},{10... | collective-permute-start | bytes 3145736 | tf_op jit(solution)/shard_map/ppermute | solution.py:12
  196.4 132.0 %all-to-all-start.2 = ((bf16[64,8,512]{2,1,0:T(8,128)(2,1)}), bf16[64,8,512]{2,1,0:T(8,128)(2,1)S(1)}, u32[]{:S(2)}, u32[]{:S(2)}) async-start(bf16[64,8,512]{2,1,0:T(8,128)(2,1)} %reduce-scatter.2.cloned.1.call-done), calls=%async_computation.3 | async-start | bytes 1048576 | tf_op jit(solution)/shard_map/all_to_all | solution.py:104
Sparse Core Ops, SparseCore 0:
  66.8 33.3 all-gather.4
  106.8 35.3 all-gather.2
  150.5 45.7 reduce-scatter.1
where the time goes:
time: 337 us
  waiting for transfers between devices  148 us (44%)
  blocking collectives  87 us (26%)
  starting transfers between devices  46.6 us (14%)
  between operations  17.9 us (5%)
  matrix products  16 us (5%)
  other arithmetic  13.6 us (4%)
  local copies, waits for them, and re-layouts  7.5 us (2%)
    ppermute x6, waiting for transfers between devices, passed_along(): return lax.ppermute(value, axis, pairs)  97.4 us
    all_to_all x1, blocking collectives, body(): lax.all_to_all(pack(jnp.repeat(layer_in, TOP, axis=0)), 'expert', split_a...  49 us
    all_to_all x1, blocking collectives, body(): lax.all_to_all(pack((prob_flat[:, None] * repeated).astype(jnp.bfloat16))...  38 us
    all_gather x1, waiting for transfers between devices, body(): lax.all_gather(lax.all_to_all(pack((prob_flat[:, None] * repeated).astype...  30.4 us
    ppermute x6, starting transfers between devices, passed_along(): return lax.ppermute(value, axis, pairs)  30.1 us
    all_to_all x1, starting transfers between devices, body(): lax.all_to_all(summed.astype(jnp.bfloat16), 'expert', split_axis=0, conca...  16.3 us
    all_to_all x1, waiting for transfers between devices, body(): lax.all_to_all(summed.astype(jnp.bfloat16), 'expert', split_axis=0, conca...  15.5 us
  transfers between devices with their start and end apart: 10, of which 7 were waited for; matrix products, arithmetic and copies ran while one was open for 5% of the time, Pallas kernels for 0%

commit v1 on v0

--- a/solution.py
+++ b/solution.py
@@ -4,6 +4,19 @@
 from jax.sharding import PartitionSpec as P
 
 TOP = 8
+
+
+def ring_gather(value, axis, dim):
+    ways = lax.axis_size(axis)
+    up = [(d, (d + 1) % ways) for d in range(ways)]
+    down = [(d, (d - 1) % ways) for d in range(ways)]
+    earlier, later = ([value], [value])
+    for _ in range(ways // 2):
+        earlier.append(lax.ppermute(earlier[-1], axis, up))
+    for _ in range((ways - 1) // 2):
+        later.append(lax.ppermute(later[-1], axis, down))
+    line = jnp.concatenate([*earlier[::-1], *later[1:]], axis=dim)
+    return jnp.roll(line, (lax.axis_index(axis) - ways // 2) * value.shape[dim], axis=dim)
 
 
 def passed_along(value, axis, steps):
@@ -60,7 +73,7 @@
             axis=2,
             tiled=True,
         ),
-        lax.all_gather(
+        ring_gather(
             lax.all_to_all(
                 pack((prob_flat[:, None] * repeated).astype(jnp.bfloat16)),
                 "expert",
@@ -69,8 +82,7 @@
                 tiled=True,
             ),
             "dp",
-            axis=2,
-            tiled=True,
+            2,
         ),
     )
     inputs = inputs.reshape(recv_rows, -1)

time: 337 us -> 352 us (1.045)
  the two profiles are of different devices: /device:TPU:32 before, /device:TPU:25 now
where the time goes in v1:
time: 352 us; the launch traced here: 351 us
  waiting for transfers between devices  142 us (40%)
  blocking collectives  84.4 us (24%)
  starting transfers between devices  57.3 us (16%)
  local copies, waits for them, and re-layouts  18.8 us (5%)
  between operations  18.3 us (5%)
  matrix products  15.6 us (4%)
  other arithmetic  14.3 us (4%)
    ppermute x6, waiting for transfers between devices, passed_along(): return lax.ppermute(value, axis, pairs)  96.2 us
    all_to_all x1, blocking collectives, body(): lax.all_to_all(pack(jnp.repeat(layer_in, TOP, axis=0)), 'expert', split_a...  47.6 us
    all_to_all x1, blocking collectives, body(): lax.all_to_all(pack((prob_flat[:, None] * repeated).astype(jnp.bfloat16))...  36.9 us
    ppermute x6, starting transfers between devices, passed_along(): return lax.ppermute(value, axis, pairs)  26.7 us
    ppermute x4, waiting for transfers between devices, ring_gather(): earlier.append(lax.ppermute(earlier[-1], axis, up))  24.8 us
    all_to_all x1, waiting for transfers between devices, body(): lax.all_to_all(summed.astype(jnp.bfloat16), 'expert', split_axis=0, conca...  21.2 us
    all_to_all x1, starting transfers between devices, body(): lax.all_to_all(summed.astype(jnp.bfloat16), 'expert', split_axis=0, conca...  15.6 us
    ppermute x4, starting transfers between devices, ring_gather(): earlier.append(lax.ppermute(earlier[-1], axis, up))  15 us
  transfers between devices with their start and end apart: 16, of which 9 were waited for; matrix products, arithmetic and copies ran while one was open for 6% of the time, Pallas kernels for 0%

profile of v1, /device:TPU:25, one launch (start us, length us, event | category | flops | bytes accessed | tf_op | source)
XLA Modules:
  0.0 351.0 jit_solution(17770139020133627076)
XLA Ops:
  17.6 47.6 %all_to_all.15 = bf16[64,8,512]{2,1,0:T(8,128)(2,1)} all-to-all(bf16[64,8,512]{2,1,0:T(8,128)(2,1)S(1)} %bitcast.69), channel_id=1, replica_groups=mesh['dp'=8,'expert'=64] {'expert'}, dimensions={0} | all-to-all | bytes 1048576 | tf_op jit(solution)/shard_map/all_to_all | solution.py:65
  68.6 36.9 %all_to_all.16 = bf16[64,8,512]{2,1,0:T(8,128)(2,1)S(1)} all-to-all(bf16[64,8,512]{2,1,0:T(8,128)(2,1)S(1)} %bitcast.70), channel_id=1, replica_groups=mesh['dp'=8,'expert'=64] {'expert'}, dimensions={0} | all-to-all | bytes 1048576 | tf_op jit(solution)/shard_map/all_to_all | solution.py:77
  105.5 3.8 %collective-permute-start = (bf16[64,8,512]{2,1,0:T(8,128)(2,1)S(1)}, bf16[64,8,512]{2,1,0:T(8,128)(2,1)S(1)}, u32[]{:S(2)}, u32[]{:S(2)}) collective-permute-start(bf16[64,8,512]{2,1,0:T(8,128)(2,1)S(1)} %all_to_all.16), channel_id=1, source_target_pairs={{0,64},{64,128},{128,192},{192,256},{256,320},{320,384},{384,448},... | collective-permute-start | bytes 1572872 | tf_op jit(solution)/shard_map/ppermute | solution.py:15
  109.3 6.1 %collective-permute-done = bf16[64,8,512]{2,1,0:T(8,128)(2,1)S(1)} collective-permute-done((bf16[64,8,512]{2,1,0:T(8,128)(2,1)S(1)}, bf16[64,8,512]{2,1,0:T(8,128)(2,1)S(1)}, u32[]{:S(2)}, u32[]{:S(2)}) %collective-permute-start) | collective-permute-done | bytes 524320 | tf_op jit(solution)/shard_map/ppermute | solution.py:15
  115.4 3.7 %collective-permute-start.1 = (bf16[64,8,512]{2,1,0:T(8,128)(2,1)S(1)}, bf16[64,8,512]{2,1,0:T(8,128)(2,1)S(1)}, u32[]{:S(2)}, u32[]{:S(2)}) collective-permute-start(bf16[64,8,512]{2,1,0:T(8,128)(2,1)S(1)} %collective-permute-done), channel_id=1, source_target_pairs={{0,64},{64,128},{128,192},{192,256},{256,320},{320,384},{384,448},... | collective-permute-start | bytes 1572872 | tf_op jit(solution)/shard_map/ppermute | solution.py:15
  119.1 6.1 %collective-permute-done.1 = bf16[64,8,512]{2,1,0:T(8,128)(2,1)S(1)} collective-permute-done((bf16[64,8,512]{2,1,0:T(8,128)(2,1)S(1)}, bf16[64,8,512]{2,1,0:T(8,128)(2,1)S(1)}, u32[]{:S(2)}, u32[]{:S(2)}) %collective-permute-start.1) | collective-permute-done | bytes 524320 | tf_op jit(solution)/shard_map/ppermute | solution.py:15
  125.2 3.7 %collective-permute-start.2 = (bf16[64,8,512]{2,1,0:T(8,128)(2,1)S(1)}, bf16[64,8,512]{2,1,0:T(8,128)(2,1)}, u32[]{:S(2)}, u32[]{:S(2)}) collective-permute-start(bf16[64,8,512]{2,1,0:T(8,128)(2,1)S(1)} %collective-permute-done.1), channel_id=1, source_target_pairs={{0,64},{64,128},{128,192},{192,256},{256,320},{320,384},{384,448},... | collective-permute-start | bytes 1572872 | tf_op jit(solution)/shard_map/ppermute | solution.py:15
  128.9 6.1 %collective-permute-done.2 = bf16[64,8,512]{2,1,0:T(8,128)(2,1)} collective-permute-done((bf16[64,8,512]{2,1,0:T(8,128)(2,1)S(1)}, bf16[64,8,512]{2,1,0:T(8,128)(2,1)}, u32[]{:S(2)}, u32[]{:S(2)}) %collective-permute-start.2) | collective-permute-done | bytes 524320 | tf_op jit(solution)/shard_map/ppermute | solution.py:15
  135.0 3.8 %collective-permute-start.3 = (bf16[64,8,512]{2,1,0:T(8,128)(2,1)}, bf16[64,8,512]{2,1,0:T(8,128)(2,1)}, u32[]{:S(2)}, u32[]{:S(2)}) collective-permute-start(bf16[64,8,512]{2,1,0:T(8,128)(2,1)} %collective-permute-done.2), channel_id=1, source_target_pairs={{0,64},{64,128},{128,192},{192,256},{256,320},{320,384},{384,448},... | collective-permute-start | bytes 1572872 | tf_op jit(solution)/shard_map/ppermute | solution.py:15
  138.8 6.4 %collective-permute-done.3 = bf16[64,8,512]{2,1,0:T(8,128)(2,1)} collective-permute-done((bf16[64,8,512]{2,1,0:T(8,128)(2,1)}, bf16[64,8,512]{2,1,0:T(8,128)(2,1)}, u32[]{:S(2)}, u32[]{:S(2)}) %collective-permute-start.3) | collective-permute-done | bytes 524320 | tf_op jit(solution)/shard_map/ppermute | solution.py:15
  153.9 3.2 copy-done.1
  158.4 3.4 fusion.1
  161.9 3.4 fusion.3
  166.6 3.3 fusion
  172.8 5.0 %collective-permute-start.10 = (bf16[128,4096]{1,0:T(8,128)(2,1)S(1)}, bf16[128,4096]{1,0:T(8,128)(2,1)}, u32[]{:S(2)}, u32[]{:S(2)}) collective-permute-start(bf16[128,4096]{1,0:T(8,128)(2,1)S(1)} %convolution_convert_fusion), channel_id=1, source_target_pairs={{0,62},{1,63},{2,0},{3,1},{4,2},{5,3},{6,4},{7,5},{8,6},{9,7},{10,... | collective-permute-start | bytes 3145736 | tf_op jit(solution)/shard_map/ppermute | solution.py:25
  179.8 8.5 %collective-permute-start.12 = (bf16[128,4096]{1,0:T(8,128)(2,1)S(1)}, bf16[128,4096]{1,0:T(8,128)(2,1)}, u32[]{:S(2)}, u32[]{:S(2)}) collective-permute-start(bf16[128,4096]{1,0:T(8,128)(2,1)S(1)} %convolution_convert_fusion), channel_id=1, source_target_pairs={{0,61},{1,62},{2,63},{3,0},{4,1},{5,2},{6,3},{7,4},{8,5},{9,6},{10... | collective-permute-start | bytes 3145736 | tf_op jit(solution)/shard_map/ppermute | solution.py:25
  190.2 6.7 %collective-permute-start.8 = (bf16[128,4096]{1,0:T(8,128)(2,1)S(1)}, bf16[128,4096]{1,0:T(8,128)(2,1)}, u32[]{:S(2)}, u32[]{:S(2)}) collective-permute-start(bf16[128,4096]{1,0:T(8,128)(2,1)S(1)} %convolution_convert_fusion), channel_id=1, source_target_pairs={{0,63},{1,0},{2,1},{3,2},{4,3},{5,4},{6,5},{7,6},{8,7},{9,8},{10,9... | collective-permute-start | bytes 3145736 | tf_op jit(solution)/shard_map/ppermute | solution.py:25
  196.9 27.5 %collective-permute-done.10 = bf16[128,4096]{1,0:T(8,128)(2,1)} collective-permute-done((bf16[128,4096]{1,0:T(8,128)(2,1)S(1)}, bf16[128,4096]{1,0:T(8,128)(2,1)}, u32[]{:S(2)}, u32[]{:S(2)}) %collective-permute-start.10) | collective-permute-done | bytes 1048608 | tf_op jit(solution)/shard_map/ppermute | solution.py:25
  227.0 15.6 %all-to-all-start.2 = ((bf16[64,8,512]{2,1,0:T(8,128)(2,1)}), bf16[64,8,512]{2,1,0:T(8,128)(2,1)S(1)}, u32[]{:S(2)}, u32[]{:S(2)}) async-start(bf16[64,8,512]{2,1,0:T(8,128)(2,1)} %reduce-scatter.2.cloned.1.call-done), calls=%async_computation.3 | async-start | bytes 1048576 | tf_op jit(solution)/shard_map/all_to_all | solution.py:116
  247.3 5.9 %collective-permute-done.11 = bf16[128,4096]{1,0:T(8,128)(2,1)} collective-permute-done((bf16[128,4096]{1,0:T(8,128)(2,1)S(1)}, bf16[128,4096]{1,0:T(8,128)(2,1)}, u32[]{:S(2)}, u32[]{:S(2)}) %collective-permute-start.11) | collective-permute-done | bytes 1048608 | tf_op jit(solution)/shard_map/ppermute | solution.py:25
  253.1 36.7 %collective-permute-done.12 = bf16[128,4096]{1,0:T(8,128)(2,1)} collective-permute-done((bf16[128,4096]{1,0:T(8,128)(2,1)S(1)}, bf16[128,4096]{1,0:T(8,128)(2,1)}, u32[]{:S(2)}, u32[]{:S(2)}) %collective-permute-start.12) | collective-permute-done | bytes 1048608 | tf_op jit(solution)/shard_map/ppermute | solution.py:25
  289.9 26.0 %collective-permute-done.8 = bf16[128,4096]{1,0:T(8,128)(2,1)} collective-permute-done((bf16[128,4096]{1,0:T(8,128)(2,1)S(1)}, bf16[128,4096]{1,0:T(8,128)(2,1)}, u32[]{:S(2)}, u32[]{:S(2)}) %collective-permute-start.8) | collective-permute-done | bytes 1048608 | tf_op jit(solution)/shard_map/ppermute | solution.py:25
  315.9 5.1 %fusion.16 = bf16[1,128,4096]{2,1,0:T(8,128)(2,1)} fusion(bf16[128,4096]{1,0:T(8,128)(2,1)} %collective-permute-done.12, f32[]{:T(128)S(6)} %convert_element_type.106, bf16[128,4096]{1,0:T(8,128)(2,1)} %collective-permute-done.11, f32[]{:T(128)S(6)} %convert_element_type.104, bf16[128,4096]{1,0:T(8,128)(2,1)} %collective-permute-done.10, ...), kind=kLoop, calls=%fused_computation.22 | loop fusion | flops 10485760 | bytes 8388632 | tf_op jit(solution)/shard_map/broadcast_in_dim | solution.py:141
  321.0 21.2 %all-to-all-done.2 = bf16[64,8,512]{2,1,0:T(8,128)(2,1)S(1)} async-done(((bf16[64,8,512]{2,1,0:T(8,128)(2,1)}), bf16[64,8,512]{2,1,0:T(8,128)(2,1)S(1)}, u32[]{:S(2)}, u32[]{:S(2)}) %all-to-all-start.2) | async-done | bytes 524320 | tf_op jit(solution)/shard_map/all_to_all | solution.py:116
  (75 shorter events, 36.9 us)
Async XLA Ops:
  7.2 151.2 %copy-start = (bf16[1,4096,128]{2,1,0:T(8,128)(2,1)S(1)}, bf16[1,4096,128]{2,1,0:T(8,128)(2,1)}, u32[]{:S(2)}) copy-start(bf16[1,4096,128]{2,1,0:T(8,128)(2,1)} %param.15) | copy-start | bytes 3145732
  7.2 151.2 %all-gather.2.cloned.1.call-start = ((), (), s32[]{:S(2)}) async-start(), calls=%async_computation.4 | async-start | bytes 4718592 | tf_op jit(solution)/shard_map/all_gather | solution.py:64
  65.2 161.8 %reduce-scatter.2.cloned.1.call-start = ((), (), s32[]{:S(2)}) async-start(), calls=%async_computation.5 | async-start | bytes 4718592 | tf_op jit(solution)/shard_map/reduce_scatter | solution.py:113
  105.5 10.0 %collective-permute-start = (bf16[64,8,512]{2,1,0:T(8,128)(2,1)S(1)}, bf16[64,8,512]{2,1,0:T(8,128)(2,1)S(1)}, u32[]{:S(2)}, u32[]{:S(2)}) collective-permute-start(bf16[64,8,512]{2,1,0:T(8,128)(2,1)S(1)} %all_to_all.16), channel_id=1, source_target_pairs={{0,64},{64,128},{128,192},{192,256},{256,320},{320,384},{384,448},... | collective-permute-start | bytes 1572872 | tf_op jit(solution)/shard_map/ppermute | solution.py:15
  115.4 9.8 %collective-permute-start.1 = (bf16[64,8,512]{2,1,0:T(8,128)(2,1)S(1)}, bf16[64,8,512]{2,1,0:T(8,128)(2,1)S(1)}, u32[]{:S(2)}, u32[]{:S(2)}) collective-permute-start(bf16[64,8,512]{2,1,0:T(8,128)(2,1)S(1)} %collective-permute-done), channel_id=1, source_target_pairs={{0,64},{64,128},{128,192},{192,256},{256,320},{320,384},{384,448},... | collective-permute-start | bytes 1572872 | tf_op jit(solution)/shard_map/ppermute | solution.py:15
  119.1 9.8 %collective-permute-start.4 = (bf16[64,8,512]{2,1,0:T(8,128)(2,1)S(1)}, bf16[64,8,512]{2,1,0:T(8,128)(2,1)S(1)}, u32[]{:S(2)}, u32[]{:S(2)}) collective-permute-start(bf16[64,8,512]{2,1,0:T(8,128)(2,1)S(1)} %all_to_all.16), channel_id=1, source_target_pairs={{0,448},{64,0},{128,64},{192,128},{256,192},{320,256},{384,320},{4... | collective-permute-start | bytes 1572872 | tf_op jit(solution)/shard_map/ppermute | solution.py:17
  125.2 9.8 %collective-permute-start.2 = (bf16[64,8,512]{2,1,0:T(8,128)(2,1)S(1)}, bf16[64,8,512]{2,1,0:T(8,128)(2,1)}, u32[]{:S(2)}, u32[]{:S(2)}) collective-permute-start(bf16[64,8,512]{2,1,0:T(8,128)(2,1)S(1)} %collective-permute-done.1), channel_id=1, source_target_pairs={{0,64},{64,128},{128,192},{192,256},{256,320},{320,384},{384,448},... | collective-permute-start | bytes 1572872 | tf_op jit(solution)/shard_map/ppermute | solution.py:15
  128.9 22.3 %copy-start.3 = (bf16[64,8,512]{2,1,0:T(8,128)(2,1)}, bf16[64,8,512]{2,1,0:T(8,128)(2,1)S(1)}, u32[]{:S(2)}) copy-start(bf16[64,8,512]{2,1,0:T(8,128)(2,1)S(1)} %collective-permute-done.4) | copy-start | bytes 1572868
  128.9 9.9 %collective-permute-start.5 = (bf16[64,8,512]{2,1,0:T(8,128)(2,1)S(1)}, bf16[64,8,512]{2,1,0:T(8,128)(2,1)}, u32[]{:S(2)}, u32[]{:S(2)}) collective-permute-start(bf16[64,8,512]{2,1,0:T(8,128)(2,1)S(1)} %collective-permute-done.4), channel_id=1, source_target_pairs={{0,448},{64,0},{128,64},{192,128},{256,192},{320,256},{384,320},{4... | collective-permute-start | bytes 1572872 | tf_op jit(solution)/shard_map/ppermute | solution.py:17
  135.0 10.2 %collective-permute-start.3 = (bf16[64,8,512]{2,1,0:T(8,128)(2,1)}, bf16[64,8,512]{2,1,0:T(8,128)(2,1)}, u32[]{:S(2)}, u32[]{:S(2)}) collective-permute-start(bf16[64,8,512]{2,1,0:T(8,128)(2,1)} %collective-permute-done.2), channel_id=1, source_target_pairs={{0,64},{64,128},{128,192},{192,256},{256,320},{320,384},{384,448},... | collective-permute-start | bytes 1572872 | tf_op jit(solution)/shard_map/ppermute | solution.py:15
  138.8 18.3 %copy-start.4 = (bf16[1,128,4096]{2,1,0:T(8,128)(2,1)S(1)}, bf16[1,128,4096]{2,1,0:T(8,128)(2,1)}, u32[]{:S(2)}) copy-start(bf16[1,128,4096]{2,1,0:T(8,128)(2,1)} %param.17) | copy-start | bytes 3145732
  138.8 10.1 %collective-permute-start.6 = (bf16[64,8,512]{2,1,0:T(8,128)(2,1)}, bf16[64,8,512]{2,1,0:T(8,128)(2,1)S(1)}, u32[]{:S(2)}, u32[]{:S(2)}) collective-permute-start(bf16[64,8,512]{2,1,0:T(8,128)(2,1)} %collective-permute-done.5), channel_id=1, source_target_pairs={{0,448},{64,0},{128,64},{192,128},{256,192},{320,256},{384,320},{4... | collective-permute-start | bytes 1572872 | tf_op jit(solution)/shard_map/ppermute | solution.py:17
  151.3 10.5 %copy-start.2 = (bf16[1,4096,128]{2,1,0:T(8,128)(2,1)S(1)}, bf16[1,4096,128]{2,1,0:T(8,128)(2,1)}, u32[]{:S(2)}) copy-start(bf16[1,4096,128]{2,1,0:T(8,128)(2,1)} %param.16) | copy-start | bytes 3145732
  153.9 3.2 copy-start.1
  172.8 51.5 %collective-permute-start.10 = (bf16[128,4096]{1,0:T(8,128)(2,1)S(1)}, bf16[128,4096]{1,0:T(8,128)(2,1)}, u32[]{:S(2)}, u32[]{:S(2)}) collective-permute-start(bf16[128,4096]{1,0:T(8,128)(2,1)S(1)} %convolution_convert_fusion), channel_id=1, source_target_pairs={{0,62},{1,63},{2,0},{3,1},{4,2},{5,3},{6,4},{7,5},{8,6},{9,7},{10,... | collective-permute-start | bytes 3145736 | tf_op jit(solution)/shard_map/ppermute | solution.py:25
  177.9 75.3 %collective-permute-start.11 = (bf16[128,4096]{1,0:T(8,128)(2,1)S(1)}, bf16[128,4096]{1,0:T(8,128)(2,1)}, u32[]{:S(2)}, u32[]{:S(2)}) collective-permute-start(bf16[128,4096]{1,0:T(8,128)(2,1)S(1)} %convolution_convert_fusion), channel_id=1, source_target_pairs={{0,3},{1,4},{2,5},{3,6},{4,7},{5,8},{6,9},{7,10},{8,11},{9,12},{10... | collective-permute-start | bytes 3145736 | tf_op jit(solution)/shard_map/ppermute | solution.py:25
  179.8 110.1 %collective-permute-start.12 = (bf16[128,4096]{1,0:T(8,128)(2,1)S(1)}, bf16[128,4096]{1,0:T(8,128)(2,1)}, u32[]{:S(2)}, u32[]{:S(2)}) collective-permute-start(bf16[128,4096]{1,0:T(8,128)(2,1)S(1)} %convolution_convert_fusion), channel_id=1, source_target_pairs={{0,61},{1,62},{2,63},{3,0},{4,1},{5,2},{6,3},{7,4},{8,5},{9,6},{10... | collective-permute-start | bytes 3145736 | tf_op jit(solution)/shard_map/ppermute | solution.py:25
  188.3 101.6 %collective-permute-start.7 = (bf16[128,4096]{1,0:T(8,128)(2,1)S(1)}, bf16[128,4096]{1,0:T(8,128)(2,1)}, u32[]{:S(2)}, u32[]{:S(2)}) collective-permute-start(bf16[128,4096]{1,0:T(8,128)(2,1)S(1)} %convolution_convert_fusion), channel_id=1, source_target_pairs={{0,1},{1,2},{2,3},{3,4},{4,5},{5,6},{6,7},{7,8},{8,9},{9,10},{10,1... | collective-permute-start | bytes 3145736 | tf_op jit(solution)/shard_map/ppermute | solution.py:25
  190.2 125.7 %collective-permute-start.8 = (bf16[128,4096]{1,0:T(8,128)(2,1)S(1)}, bf16[128,4096]{1,0:T(8,128)(2,1)}, u32[]{:S(2)}, u32[]{:S(2)}) collective-permute-start(bf16[128,4096]{1,0:T(8,128)(2,1)S(1)} %convolution_convert_fusion), channel_id=1, source_target_pairs={{0,63},{1,0},{2,1},{3,2},{4,3},{5,4},{6,5},{7,6},{8,7},{9,8},{10,9... | collective-permute-start | bytes 3145736 | tf_op jit(solution)/shard_map/ppermute | solution.py:25
  224.4 91.6 %collective-permute-start.9 = (bf16[128,4096]{1,0:T(8,128)(2,1)S(1)}, bf16[128,4096]{1,0:T(8,128)(2,1)}, u32[]{:S(2)}, u32[]{:S(2)}) collective-permute-start(bf16[128,4096]{1,0:T(8,128)(2,1)S(1)} %convolution_convert_fusion), channel_id=1, source_target_pairs={{0,2},{1,3},{2,4},{3,5},{4,6},{5,7},{6,8},{7,9},{8,10},{9,11},{10,... | collective-permute-start | bytes 3145736 | tf_op jit(solution)/shard_map/ppermute | solution.py:25
  227.0 115.2 %all-to-all-start.2 = ((bf16[64,8,512]{2,1,0:T(8,128)(2,1)}), bf16[64,8,512]{2,1,0:T(8,128)(2,1)S(1)}, u32[]{:S(2)}, u32[]{:S(2)}) async-start(bf16[64,8,512]{2,1,0:T(8,128)(2,1)} %reduce-scatter.2.cloned.1.call-done), calls=%async_computation.3 | async-start | bytes 1048576 | tf_op jit(solution)/shard_map/all_to_all | solution.py:116
Sparse Core Ops, SparseCore 0:
  65.3 33.4 all-gather.1
  170.0 38.8 reduce-scatter.1
